TPU v7x, 256 devices: a whole 4x4x8 slice. The times are simulated.
256 devices in a mesh: tm: 32 (over x, y, core), neur: 8 (over z).
Axes of the slice: x: 4, y: 4, z: 8, core: 2. Of those that a mesh axis runs over, the one named last changes fastest.
Arguments:
- activity: bfloat16 [51200, 12288], P('neur', 'tm'), may hold values from 0.01 to 1001, as said below
- patterns: bfloat16 [51200, 512], P('neur'), may hold values from 6.25e-05 to 0.08125, as said below
- loadings: bfloat16 [32, 12288], P(None, 'tm'), may hold values from 0.01 to 4.4, as said below
Outputs:
- h_next: float32 [32, 12288], P(None, 'tm')
- w_next: float32 [51200, 512], P(('neur', 'tm'))
- misfit: float32 [12288], P('tm')
Inputs may be any that keep to these rules, and one draw needn't show every extreme that they name: `activity`: positive. `patterns`: positive. `loadings`: positive.
All inputs are finite; a program needn't handle non-finite values.
Results may differ from a plain program's by a relative error of at most 0.0009.
Values may be sent and summed in bfloat16 or wider, within the bound.
A program may use at most 128 MiB of HBM per device.

v0:
```python
import jax
import jax.numpy as jnp
from jax import lax
from jax.sharding import PartitionSpec as P

RANK = 32
LAGS = 16


def passed_along(value, axis, steps):
    count = lax.axis_size(axis)
    leading, last = (max(0, -steps), min(count, count - steps))
    return lax.ppermute(value, axis, [(source, source + steps) for source in range(leading, last)])


def lag_stack(factor, rim):
    extended = jnp.concatenate([rim, factor], axis=1)
    width = factor.shape[1]
    rows = [extended[:, LAGS - 1 - lag : LAGS - 1 - lag + width] for lag in range(LAGS)]
    return jnp.concatenate(rows, axis=0)


def body(activity, patterns, loadings):
    span = loadings.shape[1]
    local_rows = patterns.shape[0]
    rim = passed_along(loadings[:, span - (LAGS - 1) :], "tm", 1)
    stacked = lag_stack(loadings, rim)
    recon = jnp.dot(patterns, stacked, preferred_element_type=jnp.float32)
    ratio = (activity.astype(jnp.float32) / recon).astype(jnp.bfloat16)
    ratio_next = passed_along(ratio[:, : LAGS - 1], "tm", -1)
    extended = jnp.concatenate([ratio, ratio_next], axis=1)
    gram = lax.dot_general(
        patterns, extended, (((0,), (0,)), ((), ())), preferred_element_type=jnp.float32
    )
    layered = gram.reshape(LAGS, RANK, span + LAGS - 1)
    numer = layered[0, :, 0:span]
    for lag in range(1, LAGS):
        numer = numer + layered[lag, :, lag : lag + span]
    colsum = jnp.sum(jnp.sum(patterns, axis=0, dtype=jnp.float32).reshape(LAGS, RANK), axis=0)
    numer_all, colsum_all = lax.psum((numer, colsum), "neur")
    h_next = loadings.astype(jnp.float32) * numer_all / colsum_all[:, None]
    fresh = h_next.astype(jnp.bfloat16)
    fresh_prev = passed_along(fresh[:, span - (LAGS - 1) :], "tm", 1)
    stacked_new = lag_stack(fresh, fresh_prev)
    act_wide = activity.astype(jnp.float32)
    recon_new = jnp.dot(patterns, stacked_new, preferred_element_type=jnp.float32)
    diverge = jnp.sum(act_wide * jnp.log(act_wide / recon_new) - act_wide + recon_new, axis=0)
    mass = jnp.sum(act_wide, axis=0)
    ratio_new = (act_wide / recon_new).astype(jnp.bfloat16)
    diverge_all, mass_all = lax.psum((diverge, mass), "neur")
    misfit = diverge_all / mass_all
    own_count = local_rows // lax.axis_size("tm")
    lag_part = jnp.sum(stacked_new, axis=1, dtype=jnp.float32)
    lagsum = lax.psum(lag_part, "tm")
    pnum = lax.psum_scatter(
        lax.dot_general(
            ratio_new, stacked_new, (((1,), (1,)), ((), ())), preferred_element_type=jnp.float32
        ),
        "tm",
        scatter_dimension=0,
        tiled=True,
    )
    own_patterns = lax.dynamic_slice_in_dim(
        patterns, lax.axis_index("tm") * own_count, own_count, 0
    )
    w_next = own_patterns.astype(jnp.float32) * pnum / lagsum[None, :]
    return (h_next, w_next, misfit)


def solution(mesh):
    return jax.shard_map(
        body,
        mesh=mesh,
        in_specs=(P("neur", "tm"), P("neur", None), P(None, "tm")),
        out_specs=(P(None, "tm"), P(("neur", "tm"), None), P("tm")),
        check_vma=False,
    )
```

profile of v0, /device:TPU:1, one launch (start us, length us, event | category | flops | bytes accessed | tf_op | source)
XLA Modules:
  0.0 218.1 jit_solution(12868446539411816418)
XLA Ops:
  7.2 0.8 slice.147
  8.0 4.6 %collective-permute-start = (bf16[32,15]{1,0:T(8,128)(2,1)S(1)}, bf16[32,15]{1,0:T(8,128)(2,1)S(1)}, u32[]{:S(2)}, u32[]{:S(2)}) collective-permute-start(bf16[32,15]{1,0:T(8,128)(2,1)S(1)} %slice.147), channel_id=1, source_target_pairs={{0,8},{8,16},{16,24},{24,32},{32,40},{40,48},{48,56},{56,64},{64,7... | collective-permute-start | bytes 2888 | tf_op jit(solution)/shard_map/ppermute | solution.py:13
  12.6 0.7 constant_dynamic-update-slice_fusion.15
  13.3 7.5 %copy.25 = bf16[6400,384]{0,1:T(8,128)(2,1)} copy(bf16[6400,384]{1,0:T(8,128)(2,1)} %param.3) | data formatting | bytes 9830400 | tf_op args[0]
  21.0 0.1 constant_dynamic-update-slice_fusion.12
  21.1 0.1 constant_dynamic-update-slice_fusion.11
  21.2 0.1 constant_dynamic-update-slice_fusion.10
  21.5 0.1 constant_dynamic-update-slice_fusion.7
  21.5 0.1 constant_dynamic-update-slice_fusion.6
  21.6 0.1 constant_dynamic-update-slice_fusion.5
  21.7 0.1 constant_dynamic-update-slice_fusion.4
  21.8 0.1 constant_dynamic-update-slice_fusion.3
  21.9 0.1 constant_dynamic-update-slice_fusion.2
  22.0 0.1 constant_dynamic-update-slice_fusion.1
  22.1 0.1 constant_dynamic-update-slice_fusion
  22.2 7.8 %fusion = bf16[6400,384]{0,1:T(8,128)(2,1)S(1)} fusion(bf16[6400,384]{0,1:T(8,128)(2,1)} %copy.25, bf16[512,384]{1,0:T(8,128)(2,1)S(1)} %constant_dynamic-update-slice_fusion, bf16[6400,512]{1,0:T(8,128)(2,1)} %param.4), kind=kOutput, calls=%fused_computation.8 | convolution fusion | flops 2523955200 | bytes 16777216 | tf_op jit(solution)/shard_map/dot_general | solution.py:28
  30.0 1.9 collective-permute-start.1
  31.9 0.3 copy-done.1
  32.2 0.9 convert_reduce_fusion.1
  33.2 3.8 %collective-permute-done.1 = bf16[6400,15]{0,1:T(8,128)(2,1)S(1)} collective-permute-done((bf16[6400,15]{0,1:T(8,128)(2,1)S(1)}, bf16[6400,15]{0,1:T(8,128)(2,1)S(1)}, u32[]{:S(2)}, u32[]{:S(2)}) %collective-permute-start.1) | collective-permute-done | bytes 192032 | tf_op jit(solution)/shard_map/ppermute | solution.py:13
  37.1 6.8 %fusion.9 = f32[512,399]{0,1:T(8,128)S(1)} fusion(bf16[6400,512]{1,0:T(8,128)(2,1)} %param.4, bf16[6400,15]{0,1:T(8,128)(2,1)S(1)} %collective-permute-done.1, bf16[6400,384]{0,1:T(8,128)(2,1)} %copy-done.1), kind=kOutput, calls=%fused_computation.17 | convolution fusion | flops 2625100800 | bytes 12477952 | tf_op jit(solution)/shard_map/dot_general | solution.py:32
  43.9 0.3 copy.26
  44.2 0.3 fusion.12
  44.5 26.0 %all-reduce.1 = (f32[32,384]{1,0:T(8,128)S(1)}, f32[32]{0:T(128)S(1)}) all-reduce(f32[32,384]{1,0:T(8,128)S(1)} %fusion.12, f32[32]{0:T(128)S(1)} %reduce_sum.46), channel_id=1, replica_groups=mesh['tm'=32,'neur'=8] {'neur'}, use_global_device_ids=true, to_apply=%region_0.0 | all-reduce | flops 12320 | bytes 98560 | tf_op jit(solution)/shard_map/psum | solution.py:40
  70.5 0.7 constant_dynamic-update-slice_fusion.31
  71.3 9.2 %collective-permute-start.2 = (bf16[32,15]{1,0:T(8,128)(2,1)S(1)}, bf16[32,15]{1,0:T(8,128)(2,1)S(1)}, u32[]{:S(2)}, u32[]{:S(2)}) collective-permute-start(bf16[32,15]{1,0:T(8,128)(2,1)S(1)} %slice.241), channel_id=1, source_target_pairs={{0,8},{8,16},{16,24},{24,32},{32,40},{40,48},{48,56},{56,64},{64,7... | collective-permute-start | bytes 2888 | tf_op jit(solution)/shard_map/ppermute | solution.py:13
  80.5 0.6 collective-permute-done.2
  81.1 0.1 constant_dynamic-update-slice_fusion.30
  81.4 0.1 constant_dynamic-update-slice_fusion.27
  81.4 0.1 constant_dynamic-update-slice_fusion.26
  81.5 0.1 constant_dynamic-update-slice_fusion.25
  81.6 0.1 constant_dynamic-update-slice_fusion.24
  81.7 0.1 constant_dynamic-update-slice_fusion.23
  81.8 0.1 constant_dynamic-update-slice_fusion.22
  81.9 0.1 constant_dynamic-update-slice_fusion.21
  82.0 0.1 constant_dynamic-update-slice_fusion.20
  82.1 0.1 constant_dynamic-update-slice_fusion.19
  82.2 0.1 constant_dynamic-update-slice_fusion.18
  82.2 0.1 constant_dynamic-update-slice_fusion.17
  82.3 0.1 constant_dynamic-update-slice_fusion.16
  82.4 7.6 %convert_reduce_fusion = (f32[384]{0:T(512)S(1)}, f32[384]{0:T(512)S(1)}, f32[6400,384]{0,1:T(8,128)S(1)}) fusion(bf16[6400,384]{0,1:T(8,128)(2,1)} %copy.25, bf16[512,384]{1,0:T(8,128)(2,1)S(1)} %constant_dynamic-update-slice_fusion.16, bf16[6400,512]{1,0:T(8,128)(2,1)} %param.4), kind=kOutput, calls=%fused_computation | convolution fusion | flops 2533784576 | bytes 21695488 | tf_op jit(solution)/shard_map/dot_general | solution.py:46
  90.1 6.8 %fusion.7 = f32[6400,512]{1,0:T(8,128)} fusion(bf16[512,384]{1,0:T(8,128)(2,1)S(1)} %constant_dynamic-update-slice_fusion.16, f32[6400,384]{0,1:T(8,128)S(1)} %get-tuple-element.12, bf16[6400,384]{0,1:T(8,128)(2,1)S(1)} %bitcast.20), kind=kOutput, calls=%fused_computation.15 | convolution fusion | flops 2523955200 | bytes 28246016 | tf_op jit(solution)/shard_map/dot_general | solution.py:56
  96.9 10.7 %all-reduce = (f32[384]{0:T(512)S(1)}, f32[384]{0:T(512)S(1)}) all-reduce(f32[384]{0:T(512)S(1)} %get-tuple-element.4, f32[384]{0:T(512)S(1)} %get-tuple-element.3), channel_id=1, replica_groups=mesh['tm'=32,'neur'=8] {'neur'}, use_global_device_ids=true, to_apply=%region_8.0 | all-reduce | flops 768 | bytes 6144 | tf_op jit(solution)/shard_map/psum | solution.py:50
  107.6 0.6 div.32
  108.2 0.1 convert_reduce_fusion.2
  108.3 67.6 %psum.37 = f32[512]{0:T(512)S(1)} all-reduce(f32[512]{0:T(512)S(1)} %convert_reduce_fusion.2), channel_id=1, replica_groups=mesh['tm'=32,'neur'=8] {'tm'}, use_global_device_ids=true, to_apply=%region_6.0 | all-reduce | flops 512 | bytes 4096 | tf_op jit(solution)/shard_map/psum | solution.py:54
  175.9 33.5 %reduce-scatter.2.cloned.1.call-done = f32[200,512]{1,0:T(8,128)} async-done(((f32[6400,512]{1,0:T(8,128)}), f32[200,512]{1,0:T(8,128)}) %reduce-scatter.2.cloned.1.call-update) | async-done | bytes 409616 | tf_op jit(solution)/shard_map/reduce_scatter | solution.py:55
  209.4 1.9 multiply_divide_fusion
  (26 shorter events, 0.8 us)
Async XLA Ops:
  7.2 13.7 %copy-start = (bf16[32,384]{1,0:T(8,128)(2,1)S(1)}, bf16[32,384]{1,0:T(8,128)(2,1)}, u32[]{:S(2)}) copy-start(bf16[32,384]{1,0:T(8,128)(2,1)} %param.5) | copy-start | bytes 73732
  7.2 202.2 %reduce-scatter.2.cloned.1.call-start = ((), (), s32[]{:S(2)}) async-start(), calls=%async_computation.1 | async-start | bytes 13516800 | tf_op jit(solution)/shard_map/reduce_scatter | solution.py:55
  8.0 12.8 %collective-permute-start = (bf16[32,15]{1,0:T(8,128)(2,1)S(1)}, bf16[32,15]{1,0:T(8,128)(2,1)S(1)}, u32[]{:S(2)}, u32[]{:S(2)}) collective-permute-start(bf16[32,15]{1,0:T(8,128)(2,1)S(1)} %slice.147), channel_id=1, source_target_pairs={{0,8},{8,16},{16,24},{24,32},{32,40},{40,48},{48,56},{56,64},{64,7... | collective-permute-start | bytes 2888 | tf_op jit(solution)/shard_map/ppermute | solution.py:13
  21.2 11.0 %slice-start = ((s8[6553600]{0:T(1024)(128)(4,1)}), s8[4194304]{0:T(1024)(128)(4,1)S(1)}, s32[]{:S(2)}) async-start(s8[6553600]{0:T(1024)(128)(4,1)} %bitcast.17), calls=%async_computation.2 | async-start | bytes 8388608
  22.2 10.1 %slice-start.1 = ((s8[6553600]{0:T(1024)(128)(4,1)}), s8[2359296]{0:T(1024)(128)(4,1)S(1)}, s32[]{:S(2)}) async-start(s8[6553600]{0:T(1024)(128)(4,1)} %bitcast.17), calls=%async_computation.3 | async-start | bytes 4718592
  30.0 2.2 %copy-start.1 = (bf16[6400,384]{0,1:T(8,128)(2,1)}, bf16[6400,384]{0,1:T(8,128)(2,1)S(1)}, u32[]{:S(2)}) copy-start(bf16[6400,384]{0,1:T(8,128)(2,1)S(1)} %fusion) | copy-start | bytes 14745604
  30.0 7.1 %collective-permute-start.1 = (bf16[6400,15]{0,1:T(8,128)(2,1)S(1)}, bf16[6400,15]{0,1:T(8,128)(2,1)S(1)}, u32[]{:S(2)}, u32[]{:S(2)}) collective-permute-start(bf16[6400,15]{0,1:T(8,128)(2,1)S(1)} %slice.224), channel_id=1, source_target_pairs={{8,0},{16,8},{24,16},{32,24},{40,32},{48,40},{56,48},{64,56},{72,6... | collective-permute-start | bytes 576008 | tf_op jit(solution)/shard_map/ppermute | solution.py:13
  44.2 45.8 %slice-start.2 = ((s8[4915200]{0:T(1024)(128)(4,1)}), s8[720896]{0:T(1024)(128)(4,1)S(1)}, s32[]{:S(2)}) async-start(s8[4915200]{0:T(1024)(128)(4,1)} %bitcast.19), calls=%async_computation.4 | async-start | bytes 1441792
  71.3 9.8 %collective-permute-start.2 = (bf16[32,15]{1,0:T(8,128)(2,1)S(1)}, bf16[32,15]{1,0:T(8,128)(2,1)S(1)}, u32[]{:S(2)}, u32[]{:S(2)}) collective-permute-start(bf16[32,15]{1,0:T(8,128)(2,1)S(1)} %slice.241), channel_id=1, source_target_pairs={{0,8},{8,16},{16,24},{24,32},{32,40},{40,48},{48,56},{56,64},{64,7... | collective-permute-start | bytes 2888 | tf_op jit(solution)/shard_map/ppermute | solution.py:13
  82.4 7.7 %slice-start.3 = ((s8[4915200]{0:T(1024)(128)(4,1)}), s8[4194304]{0:T(1024)(128)(4,1)S(1)}, s32[]{:S(2)}) async-start(s8[4915200]{0:T(1024)(128)(4,1)} %bitcast.19), calls=%async_computation.5 | async-start | bytes 8388608
Sparse Core Ops, SparseCore 0:
  97.0 112.3 reduce-scatter.1
where the time goes:
time: 219 us; the launch traced here: 218 us
  blocking collectives  104 us (47%)
  waiting for transfers between devices  38 us (17%)
  matrix products  29 us (13%)
  starting transfers between devices  15.8 us (7%)
  between operations  14.2 us (6%)
  local copies, waits for them, and re-layouts  9.82 us (4%)
  other arithmetic  7.12 us (3%)
    psum x1, blocking collectives, body(): lagsum = lax.psum(lag_part, 'tm')  67.6 us
    reduce_scatter x1, waiting for transfers between devices, body(): lax.psum_scatter(lax.dot_general(ratio_new, stacked_new, (((1,), (1,)), (...  33.5 us
    psum x1, blocking collectives, body(): numer_all, colsum_all = lax.psum((numer, colsum), 'neur')  26 us
    ppermute x3, starting transfers between devices, passed_along(): lax.ppermute(value, axis, [(source, source + steps) for source in range(l...  15.7 us
    psum x1, blocking collectives, body(): diverge_all, mass_all = lax.psum((diverge, mass), 'neur')  10.7 us
    unnamed x14, local copies, waits for them, and re-layouts  8.53 us
    dot_general x1, matrix products, body(): recon = jnp.dot(patterns, stacked, preferred_element_type=jnp.float32)  7.79 us
    dot_general x1, matrix products, body(): jnp.dot(patterns, stacked_new, preferred_element_type=jnp.float32)  7.64 us
  transfers between devices with their start and end apart: 4, of which 3 were waited for; matrix products, arithmetic and copies ran while one was open for 5% of the time, Pallas kernels for 0%

commit v1 on v0

--- a/solution.py
+++ b/solution.py
@@ -51,7 +51,7 @@
     misfit = diverge_all / mass_all
     own_count = local_rows // lax.axis_size("tm")
     lag_part = jnp.sum(stacked_new, axis=1, dtype=jnp.float32)
-    lagsum = lax.psum(lag_part, "tm")
+    lagsum = jnp.sum(lax.all_gather(lag_part, "tm"), 0)
     pnum = lax.psum_scatter(
         lax.dot_general(
             ratio_new, stacked_new, (((1,), (1,)), ((), ())), preferred_element_type=jnp.float32

time: 219 us -> 219 us (level)
  waiting for transfers between devices: 38 us -> 76.6 us
  blocking collectives: 104 us -> 65.6 us
    psum x1 -> x0, blocking collectives: 67.6 us -> none  [body(): lagsum = lax.psum(lag_part, 'tm')]
    reduce_scatter x1, waiting for transfers between devices: 33.5 us -> 72.1 us  [body(): lax.psum_scatter(lax.dot_general(ratio_new, stacked_new, (((1,), (1,)), (...]
    all_gather x0 -> x1, blocking collectives: none -> 28.9 us  [body(): lagsum = jnp.sum(lax.all_gather(lag_part, 'tm'), 0)]
where the time goes in v1:
time: 219 us; the launch traced here: 218 us
  waiting for transfers between devices  76.6 us (35%)
  blocking collectives  65.6 us (30%)
  matrix products  29 us (13%)
  starting transfers between devices  15.8 us (7%)
  between operations  14.2 us (6%)
  local copies, waits for them, and re-layouts  9.82 us (4%)
  other arithmetic  7.19 us (3%)
    reduce_scatter x1, waiting for transfers between devices, body(): lax.psum_scatter(lax.dot_general(ratio_new, stacked_new, (((1,), (1,)), (...  72.1 us
    all_gather x1, blocking collectives, body(): lagsum = jnp.sum(lax.all_gather(lag_part, 'tm'), 0)  28.9 us
    psum x1, blocking collectives, body(): numer_all, colsum_all = lax.psum((numer, colsum), 'neur')  26 us
    ppermute x3, starting transfers between devices, passed_along(): lax.ppermute(value, axis, [(source, source + steps) for source in range(l...  15.7 us
    psum x1, blocking collectives, body(): diverge_all, mass_all = lax.psum((diverge, mass), 'neur')  10.7 us
    unnamed x14, local copies, waits for them, and re-layouts  8.53 us
    dot_general x1, matrix products, body(): recon = jnp.dot(patterns, stacked, preferred_element_type=jnp.float32)  7.79 us
    dot_general x1, matrix products, body(): jnp.dot(patterns, stacked_new, preferred_element_type=jnp.float32)  7.72 us
  transfers between devices with their start and end apart: 4, of which 3 were waited for; matrix products, arithmetic and copies ran while one was open for 5% of the time, Pallas kernels for 0%

profile of v1, /device:TPU:1, one launch (start us, length us, event | category | flops | bytes accessed | tf_op | source)
XLA Modules:
  0.0 218.2 jit_solution(2674022671627347716)
XLA Ops:
  7.2 0.8 slice.147
  8.0 4.6 %collective-permute-start = (bf16[32,15]{1,0:T(8,128)(2,1)S(1)}, bf16[32,15]{1,0:T(8,128)(2,1)S(1)}, u32[]{:S(2)}, u32[]{:S(2)}) collective-permute-start(bf16[32,15]{1,0:T(8,128)(2,1)S(1)} %slice.147), channel_id=1, source_target_pairs={{0,8},{8,16},{16,24},{24,32},{32,40},{40,48},{48,56},{56,64},{64,7... | collective-permute-start | bytes 2888 | tf_op jit(solution)/shard_map/ppermute | solution.py:13
  12.6 0.7 constant_dynamic-update-slice_fusion.15
  13.3 7.5 %copy.27 = bf16[6400,384]{0,1:T(8,128)(2,1)} copy(bf16[6400,384]{1,0:T(8,128)(2,1)} %param.3) | data formatting | bytes 9830400 | tf_op args[0]
  21.0 0.1 constant_dynamic-update-slice_fusion.12
  21.1 0.1 constant_dynamic-update-slice_fusion.11
  21.2 0.1 constant_dynamic-update-slice_fusion.10
  21.4 0.1 constant_dynamic-update-slice_fusion.8
  21.5 0.1 constant_dynamic-update-slice_fusion.7
  21.5 0.1 constant_dynamic-update-slice_fusion.6
  21.6 0.1 constant_dynamic-update-slice_fusion.5
  21.7 0.1 constant_dynamic-update-slice_fusion.4
  21.8 0.1 constant_dynamic-update-slice_fusion.3
  21.9 0.1 constant_dynamic-update-slice_fusion.2
  22.0 0.1 constant_dynamic-update-slice_fusion.1
  22.1 0.1 constant_dynamic-update-slice_fusion
  22.2 7.8 %fusion = bf16[6400,384]{0,1:T(8,128)(2,1)S(1)} fusion(bf16[6400,384]{0,1:T(8,128)(2,1)} %copy.27, bf16[512,384]{1,0:T(8,128)(2,1)S(1)} %constant_dynamic-update-slice_fusion, bf16[6400,512]{1,0:T(8,128)(2,1)} %param.4), kind=kOutput, calls=%fused_computation.8 | convolution fusion | flops 2523955200 | bytes 16777216 | tf_op jit(solution)/shard_map/dot_general | solution.py:28
  30.0 1.9 collective-permute-start.1
  31.9 0.3 copy-done.1
  32.2 0.9 convert_reduce_fusion.1
  33.2 3.8 %collective-permute-done.1 = bf16[6400,15]{0,1:T(8,128)(2,1)S(1)} collective-permute-done((bf16[6400,15]{0,1:T(8,128)(2,1)S(1)}, bf16[6400,15]{0,1:T(8,128)(2,1)S(1)}, u32[]{:S(2)}, u32[]{:S(2)}) %collective-permute-start.1) | collective-permute-done | bytes 192032 | tf_op jit(solution)/shard_map/ppermute | solution.py:13
  37.1 6.8 %fusion.9 = f32[512,399]{0,1:T(8,128)S(1)} fusion(bf16[6400,512]{1,0:T(8,128)(2,1)} %param.4, bf16[6400,15]{0,1:T(8,128)(2,1)S(1)} %collective-permute-done.1, bf16[6400,384]{0,1:T(8,128)(2,1)} %copy-done.1), kind=kOutput, calls=%fused_computation.17 | convolution fusion | flops 2625100800 | bytes 12477952 | tf_op jit(solution)/shard_map/dot_general | solution.py:32
  43.9 0.3 copy.28
  44.2 0.3 fusion.12
  44.5 26.0 %all-reduce.1 = (f32[32,384]{1,0:T(8,128)S(1)}, f32[32]{0:T(128)S(1)}) all-reduce(f32[32,384]{1,0:T(8,128)S(1)} %fusion.12, f32[32]{0:T(128)S(1)} %reduce_sum.55), channel_id=1, replica_groups=mesh['tm'=32,'neur'=8] {'neur'}, use_global_device_ids=true, to_apply=%region_0.0 | all-reduce | flops 12320 | bytes 98560 | tf_op jit(solution)/shard_map/psum | solution.py:40
  70.5 0.7 constant_dynamic-update-slice_fusion.31
  71.2 9.2 %collective-permute-start.2 = (bf16[32,15]{1,0:T(8,128)(2,1)S(1)}, bf16[32,15]{1,0:T(8,128)(2,1)S(1)}, u32[]{:S(2)}, u32[]{:S(2)}) collective-permute-start(bf16[32,15]{1,0:T(8,128)(2,1)S(1)} %slice.241), channel_id=1, source_target_pairs={{0,8},{8,16},{16,24},{24,32},{32,40},{40,48},{48,56},{56,64},{64,7... | collective-permute-start | bytes 2888 | tf_op jit(solution)/shard_map/ppermute | solution.py:13
  80.5 0.6 collective-permute-done.2
  81.3 0.1 constant_dynamic-update-slice_fusion.27
  81.4 0.1 constant_dynamic-update-slice_fusion.26
  81.5 0.1 constant_dynamic-update-slice_fusion.25
  81.6 0.1 constant_dynamic-update-slice_fusion.24
  81.7 0.1 constant_dynamic-update-slice_fusion.23
  81.8 0.1 constant_dynamic-update-slice_fusion.22
  81.9 0.1 constant_dynamic-update-slice_fusion.21
  81.9 0.1 constant_dynamic-update-slice_fusion.20
  82.0 0.1 constant_dynamic-update-slice_fusion.19
  82.1 0.1 constant_dynamic-update-slice_fusion.18
  82.2 0.1 constant_dynamic-update-slice_fusion.17
  82.3 0.1 constant_dynamic-update-slice_fusion.16
  82.4 7.7 %convert_reduce_fusion = (f32[384]{0:T(512)S(1)}, f32[384]{0:T(512)S(1)}, f32[6400,384]{0,1:T(8,128)S(1)}) fusion(bf16[6400,384]{0,1:T(8,128)(2,1)} %copy.27, bf16[512,384]{1,0:T(8,128)(2,1)S(1)} %constant_dynamic-update-slice_fusion.16, bf16[6400,512]{1,0:T(8,128)(2,1)} %param.4), kind=kOutput, calls=%fused_computation | convolution fusion | flops 2533784576 | bytes 21695488 | tf_op jit(solution)/shard_map/dot_general | solution.py:46
  90.1 6.8 %fusion.7 = f32[6400,512]{1,0:T(8,128)} fusion(bf16[512,384]{1,0:T(8,128)(2,1)S(1)} %constant_dynamic-update-slice_fusion.16, f32[6400,384]{0,1:T(8,128)S(1)} %get-tuple-element.12, bf16[6400,384]{0,1:T(8,128)(2,1)S(1)} %bitcast.21), kind=kOutput, calls=%fused_computation.15 | convolution fusion | flops 2523955200 | bytes 28246016 | tf_op jit(solution)/shard_map/dot_general | solution.py:56
  96.9 0.1 convert_reduce_fusion.2
  97.1 28.9 %all-gather.1 = f32[32,1,512]{2,1,0:T(1,128)S(1)} all-gather(f32[1,1,512]{2,1,0:T(1,128)S(1)} %bitcast.23), channel_id=2, replica_groups=mesh['tm'=32,'neur'=8] {'tm'}, dimensions={0}, use_global_device_ids=true | all-gather | bytes 67584 | tf_op jit(solution)/shard_map/all_gather | solution.py:54
  126.1 10.7 %all-reduce = (f32[384]{0:T(512)S(1)}, f32[384]{0:T(512)S(1)}) all-reduce(f32[384]{0:T(512)S(1)} %get-tuple-element.4, f32[384]{0:T(512)S(1)} %get-tuple-element.3), channel_id=1, replica_groups=mesh['tm'=32,'neur'=8] {'neur'}, use_global_device_ids=true, to_apply=%region_8.0 | all-reduce | flops 768 | bytes 6144 | tf_op jit(solution)/shard_map/psum | solution.py:50
  136.8 0.6 div.32
  137.4 72.1 %reduce-scatter.2.cloned.1.call-done = f32[200,512]{1,0:T(8,128)} async-done(((f32[6400,512]{1,0:T(8,128)}), f32[200,512]{1,0:T(8,128)}) %reduce-scatter.2.cloned.1.call-update) | async-done | bytes 409616 | tf_op jit(solution)/shard_map/reduce_scatter | solution.py:55
  209.5 1.9 multiply_divide_fusion
  (27 shorter events, 0.9 us)
Async XLA Ops:
  7.2 13.7 %copy-start = (bf16[32,384]{1,0:T(8,128)(2,1)S(1)}, bf16[32,384]{1,0:T(8,128)(2,1)}, u32[]{:S(2)}) copy-start(bf16[32,384]{1,0:T(8,128)(2,1)} %param.5) | copy-start | bytes 73732
  7.2 202.3 %reduce-scatter.2.cloned.1.call-start = ((), (), s32[]{:S(2)}) async-start(), calls=%async_computation.1 | async-start | bytes 13516800 | tf_op jit(solution)/shard_map/reduce_scatter | solution.py:55
  8.0 12.8 %collective-permute-start = (bf16[32,15]{1,0:T(8,128)(2,1)S(1)}, bf16[32,15]{1,0:T(8,128)(2,1)S(1)}, u32[]{:S(2)}, u32[]{:S(2)}) collective-permute-start(bf16[32,15]{1,0:T(8,128)(2,1)S(1)} %slice.147), channel_id=1, source_target_pairs={{0,8},{8,16},{16,24},{24,32},{32,40},{40,48},{48,56},{56,64},{64,7... | collective-permute-start | bytes 2888 | tf_op jit(solution)/shard_map/ppermute | solution.py:13
  21.2 11.0 %slice-start = ((s8[6553600]{0:T(1024)(128)(4,1)}), s8[4194304]{0:T(1024)(128)(4,1)S(1)}, s32[]{:S(2)}) async-start(s8[6553600]{0:T(1024)(128)(4,1)} %bitcast.18), calls=%async_computation.2 | async-start | bytes 8388608
  22.2 10.1 %slice-start.1 = ((s8[6553600]{0:T(1024)(128)(4,1)}), s8[2359296]{0:T(1024)(128)(4,1)S(1)}, s32[]{:S(2)}) async-start(s8[6553600]{0:T(1024)(128)(4,1)} %bitcast.18), calls=%async_computation.3 | async-start | bytes 4718592
  30.0 2.2 %copy-start.1 = (bf16[6400,384]{0,1:T(8,128)(2,1)}, bf16[6400,384]{0,1:T(8,128)(2,1)S(1)}, u32[]{:S(2)}) copy-start(bf16[6400,384]{0,1:T(8,128)(2,1)S(1)} %fusion) | copy-start | bytes 14745604
  30.0 7.1 %collective-permute-start.1 = (bf16[6400,15]{0,1:T(8,128)(2,1)S(1)}, bf16[6400,15]{0,1:T(8,128)(2,1)S(1)}, u32[]{:S(2)}, u32[]{:S(2)}) collective-permute-start(bf16[6400,15]{0,1:T(8,128)(2,1)S(1)} %slice.224), channel_id=1, source_target_pairs={{8,0},{16,8},{24,16},{32,24},{40,32},{48,40},{56,48},{64,56},{72,6... | collective-permute-start | bytes 576008 | tf_op jit(solution)/shard_map/ppermute | solution.py:13
  44.2 45.9 %slice-start.2 = ((s8[4915200]{0:T(1024)(128)(4,1)}), s8[720896]{0:T(1024)(128)(4,1)S(1)}, s32[]{:S(2)}) async-start(s8[4915200]{0:T(1024)(128)(4,1)} %bitcast.20), calls=%async_computation.4 | async-start | bytes 1441792
  71.2 9.8 %collective-permute-start.2 = (bf16[32,15]{1,0:T(8,128)(2,1)S(1)}, bf16[32,15]{1,0:T(8,128)(2,1)S(1)}, u32[]{:S(2)}, u32[]{:S(2)}) collective-permute-start(bf16[32,15]{1,0:T(8,128)(2,1)S(1)} %slice.241), channel_id=1, source_target_pairs={{0,8},{8,16},{16,24},{24,32},{32,40},{40,48},{48,56},{56,64},{64,7... | collective-permute-start | bytes 2888 | tf_op jit(solution)/shard_map/ppermute | solution.py:13
  82.4 7.7 %slice-start.3 = ((s8[4915200]{0:T(1024)(128)(4,1)}), s8[4194304]{0:T(1024)(128)(4,1)S(1)}, s32[]{:S(2)}) async-start(s8[4915200]{0:T(1024)(128)(4,1)} %bitcast.20), calls=%async_computation.5 | async-start | bytes 8388608
Sparse Core Ops, SparseCore 0:
  97.0 112.3 reduce-scatter.1
